TPU v7x, 32 devices: a whole 2x2x4 slice. The times are simulated.
32 devices in a mesh: pocket: 16 (over z, y, x), tensor: 2 (over core).
Axes of the slice: x: 2, y: 2, z: 4, core: 2. Of those that a mesh axis runs over, the one named last changes fastest.
Arguments:
- z_home: bfloat16 [48, 32, 256], P('pocket'), may hold values from -6 to 6
- counts: int32 [48], replicated, may hold values from 1 to 32, as said below
- table: int32 [48, 32], replicated, may hold values from 0 to 575, as said below
- keys: bfloat16 [48, 1536, 128], P('pocket', 'tensor'), may hold values from -2500 to 2500, as said below
- values: bfloat16 [48, 1536, 128], P('pocket', 'tensor'), may hold values from -6 to 6
- w_embed: float32 [16, 1536], replicated, may hold values from -1.5 to 1.5
- step_bias: float32 [4, 1536], replicated, may hold values from -6 to 6
- ln_gain: float32 [1536], replicated, may hold values from 0.1 to 1.9
- w_query: bfloat16 [1536, 1536], P('tensor'), may hold values from -0.15625 to 0.15625
- w_out: bfloat16 [1536, 16], P('tensor'), may hold values from -0.15625 to 0.15625
Outputs:
- denoised: float32 [576, 256], P('pocket')
Inputs may be any that keep to these rules, and one draw needn't show every extreme that they name: `counts`: each pocket holds 1 to 32 samples. On half of the devices of the pocket axis the 3 pockets of a device hold 44 samples together, one of them exactly 32; on the other half they hold 28. `table`: positions s < counts[p] of pocket p are live and name distinct work slots that cover all 576; slot g lies on device g // 36 of the pocket axis. Entries at other positions are arbitrary and unused. A device keeps its own live samples up to 36; a device with 44 hands exactly one sample to each device that holds 28, and no device hands more than 1 to another. `keys`: finite values.
All inputs are finite; a program needn't handle non-finite values.
Results may differ from a plain program's by a relative error of at most 0.017.
The roundings to bfloat16 on the way count: a program that leaves them out, or rounds other values in their place, can miss the bound.
Values may be sent and summed in bfloat16 or wider, within the bound.
A program may use at most 64 MiB of HBM per device.

v0:
```python
import functools

import jax
import jax.numpy as jnp
from jax import lax
from jax.experimental import pallas as pl
from jax.experimental.pallas import tpu as pltpu
from jax.sharding import PartitionSpec as P

HEAD = 64
CAP = 1
WORK = 36
GS = 8
EPS = 1e-05
F32 = jnp.float32
BF16 = jnp.bfloat16
HIGHEST = lax.Precision.HIGHEST
NT = (((1,), (1,)), ((), ()))
TN = (((0,), (0,)), ((), ()))


def iota(shape, axis):
    return lax.broadcasted_iota(jnp.int32, shape, axis)


def split3(value):
    high = value.astype(BF16).astype(F32)
    rest = value - high
    middle = rest.astype(BF16).astype(F32)
    return high, middle, rest - middle


def kernel(
    dims,
    counts_s, counts_v, table_ref, z_home_ref, keys_ref, values_ref, w_embed_ref, step_bias_ref,
    gain_ref, w_query_ref, w_out_ref, out_ref,
    zf, kbd, vbd, wr, wo, z_ref, normed, queries, attended, part, send, recv,
    psend, precv, fsend, frecv,
):
    nodes, tensors, groups, halves, steps, smax, pdev = dims
    me = lax.axis_index("pocket")
    mt = lax.axis_index("tensor")
    width = w_embed_ref.shape[1]
    channels = w_embed_ref.shape[0]
    atoms = z_home_ref.shape[2] // channels
    local = w_query_ref.shape[0]
    pairs = local // (2 * HEAD)
    rows = GS * atoms
    per = smax // GS
    pockets = nodes * pdev

    barrier = pltpu.get_barrier_semaphore()
    for k in range(1, nodes):
        pl.semaphore_signal(barrier, 1, device_id=(lax.rem(me + k, nodes), mt), device_id_type=pl.DeviceIdType.MESH)
    for k in range(1, tensors):
        pl.semaphore_signal(barrier, 1, device_id=(me, lax.rem(mt + k, tensors)), device_id_type=pl.DeviceIdType.MESH)

    tops = []
    total = 0
    for p in range(pdev):
        total = total + (counts_s[me * pdev + p] + (GS - 1)) // GS
        tops.append(total)

    def place(g):
        pocket = jnp.int32(0)
        first = jnp.int32(0)
        for p in range(pdev - 1):
            past = g >= tops[p]
            pocket = jnp.where(past, p + 1, pocket)
            first = jnp.where(past, tops[p], first)
        block = jnp.clip(g - first, 0, per - 1)
        return pocket, pocket * per + block

    w_full = w_embed_ref[...]
    w_mid = w_full - jnp.mean(w_full, axis=1, keepdims=True)
    a, b, c = split3(w_mid)
    w_six = [v.astype(BF16) for v in (a, b, c, a, b, a)]
    bias = step_bias_ref[...]
    bias = bias - jnp.mean(bias, axis=1, keepdims=True)
    ba, bb, bc = split3(bias)
    row_id = iota((channels, width), 0)
    for t in range(steps):
        for k in range(6):
            wr[t, k * channels:(k + 1) * channels, :] = w_six[k]
        block = jnp.where(row_id == 0, ba[t:t + 1], jnp.where(row_id == 1, bb[t:t + 1], jnp.where(row_id == 2, bc[t:t + 1], 0.0)))
        wr[t, 6 * channels:7 * channels, :] = block.astype(BF16)
        wr[t, 7 * channels:, :] = jnp.zeros((128 - 7 * channels, width), BF16)
    spread = (iota((channels, 128), 0) == lax.rem(iota((channels, 128), 1), channels)).astype(BF16)
    wo[...] = jnp.dot(w_out_ref[...], spread, preferred_element_type=F32).astype(BF16)

    residues = keys_ref.shape[2]
    top = iota((2 * HEAD, residues), 0) < HEAD
    ones = (
        (iota((2 * residues, 2 * HEAD), 0) < residues) == (iota((2 * residues, 2 * HEAD), 1) < HEAD)
    ).astype(F32).astype(BF16)

    def prepare(i, carry):
        p = i // pairs
        hp = lax.rem(i, pairs)
        start = pl.multiple_of(hp * 2 * HEAD, 2 * HEAD)
        k_pair = keys_ref[p, pl.ds(start, 2 * HEAD), :].astype(F32) * 0.125
        kbd[i, :, :residues] = jnp.where(top, k_pair, 0.0).astype(BF16)
        kbd[i, :, residues:] = jnp.where(top, 0.0, k_pair).astype(BF16)
        v_pair = values_ref[p, pl.ds(start, 2 * HEAD), :].astype(F32)
        vbd[i, :residues, :2 * HEAD] = jnp.where(top, v_pair, 0.0).T.astype(BF16)
        vbd[i, residues:, :2 * HEAD] = jnp.where(top, 0.0, v_pair).T.astype(BF16)
        vbd[i, :, 2 * HEAD:] = ones
        return carry

    lax.fori_loop(0, pdev * pairs, prepare, 0)

    for p in range(pdev):
        block = z_home_ref[p].astype(F32)
        for j in range(per):
            zf[p * per + j] = block[j * GS:(j + 1) * GS]

    flat = atoms * channels
    own_atom = iota((rows, flat), 1) // channels == lax.rem(iota((rows, flat), 0), atoms)
    fold = (lax.rem(iota((flat, 128), 0), channels) == lax.rem(iota((flat, 128), 1), channels)).astype(BF16)
    for g in range(groups):
        pocket, block = place(jnp.int32(g))
        flat_z = zf[block]
        copies = jnp.broadcast_to(flat_z[:, None, :], (GS, atoms, flat)).reshape(rows, flat)
        copies = jnp.where(own_atom, copies, 0.0).astype(BF16)
        z_ref[g * rows:(g + 1) * rows, :] = jnp.dot(copies, fold, preferred_element_type=F32)

    pl.semaphore_wait(barrier, nodes + tensors - 2)

    lane = iota((rows, 128), 1)
    gain = gain_ref[...]

    def exchange(t, h, k):
        first, count = halves[h]
        here = part.at[t, mt, first * rows:(first + count) * rows, :]
        return pltpu.make_async_remote_copy(
            src_ref=here, dst_ref=here, send_sem=psend.at[t, h, k - 1], recv_sem=precv.at[t, h, k - 1],
            device_id=(me, lax.rem(mt + k, tensors)), device_id_type=pl.DeviceIdType.MESH,
        )

    def pick(t, table):
        value = jnp.float32(table[-1])
        for k in range(steps - 1):
            value = jnp.where(t == k, jnp.float32(table[k]), value)
        return value

    keeps = [0.95 + 0.01 * k for k in range(steps)]
    pushes = [-0.8 + 0.1 * k for k in range(steps)]

    def update(t, h):
        first, count = halves[h]
        for k in range(1, tensors):
            exchange(t, h, k).wait()
        window = slice(first * rows, (first + count) * rows)
        guess = part[t, 0, window, :]
        for k in range(1, tensors):
            guess = guess + part[t, k, window, :]
        z_ref[window, :] = pick(t, keeps) * z_ref[window, :] + pick(t, pushes) * guess

    def compute(t, h):
        first, count = halves[h]

        def embed(i, carry):
            start = pl.multiple_of((first + i) * rows, rows)
            high, middle, low = split3(z_ref[pl.ds(start, rows), :])
            left = jnp.where(lane < 3 * channels, high, jnp.where(lane < 5 * channels, middle, jnp.where(lane < 6 * channels, low, 1.0)))
            centred = jnp.dot(left.astype(BF16), wr[t], preferred_element_type=F32)
            variance = jnp.sum(centred * centred, axis=1, keepdims=True) * (1.0 / width)
            normed[pl.ds(start, rows), :] = (centred * lax.rsqrt(variance + EPS) * gain).astype(BF16)
            return carry

        lax.fori_loop(0, count, embed, 0)
        window = slice(first * rows, (first + count) * rows)
        queries[window, :] = lax.dot_general(
            normed[window, :], w_query_ref[...], NT, preferred_element_type=F32
        ).astype(BF16)

        def attend(i, carry):
            g = first + i
            start = pl.multiple_of(g * rows, rows)
            pocket, _ = place(g)
            for hp in range(pairs):
                cols = slice(hp * 2 * HEAD, (hp + 1) * 2 * HEAD)
                scores = jnp.dot(queries[pl.ds(start, rows), cols], kbd[pocket * pairs + hp], preferred_element_type=F32)
                s0 = scores[:, :residues]
                s1 = scores[:, residues:]
                e0 = jnp.exp(s0 - jnp.max(s0, axis=1, keepdims=True))
                e1 = jnp.exp(s1 - jnp.max(s1, axis=1, keepdims=True))
                e = jnp.concatenate([e0.astype(BF16), e1.astype(BF16)], axis=1)
                mixed = jnp.dot(e, vbd[pocket * pairs + hp], preferred_element_type=F32)
                attended[pl.ds(start, rows), cols] = (mixed[:, :2 * HEAD] / mixed[:, 2 * HEAD:]).astype(BF16)
            return carry

        lax.fori_loop(0, count, attend, 0)
        part[t, mt, window, :] = jnp.dot(attended[window, :], wo[...], preferred_element_type=F32)
        for k in range(1, tensors):
            exchange(t, h, k).start()

    for h in range(len(halves)):
        compute(0, h)

    def step(t, carry):
        for h in range(len(halves)):
            update(t - 1, h)
            compute(t, h)
        return carry

    lax.fori_loop(1, steps, step, 0)

    seats = groups * GS
    slots = -(-WORK // 8) * 8
    lanes = iota((1, seats), 1)
    entry = jnp.full((1, seats), -1, jnp.int32)
    for g in range(groups):
        _, block = place(jnp.int32(g))
        inside = (lanes >= g * GS) & (lanes < (g + 1) * GS) & (g < tops[-1])
        entry = jnp.where(inside, block * GS + lanes - g * GS, entry)
    keep_rows = jnp.zeros((slots, seats), F32)
    send_rows = jnp.zeros((nodes, seats), F32)
    for p in range(pdev):
        target = table_ref[pl.ds(me * pdev + p, 1), :]
        alive = iota((1, smax), 1) < counts_s[me * pdev + p]
        target = jnp.where(alive, target, -1)
        matches = (iota((smax, seats), 0) + p * smax == entry).astype(F32)
        stay = (iota((slots, smax), 0) == target - me * WORK) & (iota((slots, smax), 0) < WORK)
        keep_rows = keep_rows + jnp.dot(stay.astype(F32), matches, preferred_element_type=F32)
        node = iota((nodes, smax), 0)
        leave = (target >= node * WORK) & (target < node * WORK + WORK) & (node != me)
        send_rows = send_rows + jnp.dot(leave.astype(F32), matches, preferred_element_type=F32)
    diagonal = iota((pockets, pockets), 0) == iota((pockets, pockets), 1)
    count_rows = jnp.sum(jnp.where(diagonal, counts_v[...].astype(F32), 0.0), axis=1, keepdims=True)
    here = table_ref[...] - me * WORK
    whose = iota((pockets, smax), 0)
    arrives = (
        (iota((pockets, smax), 1).astype(F32) < count_rows)
        & (here >= 0) & (here < WORK)
        & ((whose < me * pdev) | (whose >= me * pdev + pdev))
    )
    arrival = jnp.max(jnp.where(arrives, here.astype(F32), -1.0), axis=1, keepdims=True)
    by_pocket = (arrival == iota((pockets, slots), 1).astype(F32)).astype(F32)
    pocket_id = iota((pockets, nodes), 0)
    node_id = iota((pockets, nodes), 1) * pdev
    by_node = ((pocket_id >= node_id) & (pocket_id < node_id + pdev)).astype(F32)
    take_rows = lax.dot_general(by_pocket, by_node, TN, preferred_element_type=F32)

    for h in range(len(halves)):
        update(steps - 1, h)
    done = []
    for g in range(groups):
        z = z_ref[g * rows:(g + 1) * rows, :]
        wide = jnp.concatenate([z] * (flat // 128), axis=1)
        done.append(jnp.sum(jnp.where(own_atom, wide, 0.0).reshape(GS, atoms, flat), axis=1))
    done = jnp.concatenate(done, axis=0)
    leaving = jnp.dot(send_rows, done, precision=HIGHEST, preferred_element_type=F32)
    for d in range(nodes):
        send[d] = leaving[d:d + 1]

    def hand(k):
        peer = lax.rem(me + k, nodes)
        return pltpu.make_async_remote_copy(
            src_ref=send.at[peer], dst_ref=recv.at[me], send_sem=fsend.at[k - 1], recv_sem=frecv.at[k - 1],
            device_id=(peer, mt), device_id_type=pl.DeviceIdType.MESH,
        )

    for k in range(1, nodes):
        hand(k).start()
    recv[me] = jnp.zeros((1, flat), F32)
    result = jnp.dot(keep_rows, done, precision=HIGHEST, preferred_element_type=F32)
    for k in range(1, nodes):
        hand(k).wait()
    landed = recv[...].reshape(nodes, flat)
    result = result + jnp.dot(take_rows, landed, precision=HIGHEST, preferred_element_type=F32)
    out_ref[...] = result[:WORK]


def per_device(z_home, counts, table, keys, values, w_embed, step_bias, ln_gain, w_query, w_out):
    nodes = lax.axis_size("pocket")
    tensors = lax.axis_size("tensor")
    pdev, smax, flat = z_home.shape
    channels, width = w_embed.shape
    atoms = flat // channels
    steps = step_bias.shape[0]
    local = w_query.shape[0]
    pairs = local // (2 * HEAD)
    residues = keys.shape[2]
    heavy = WORK + CAP * nodes // 2
    light = WORK - CAP * nodes // 2
    groups = max(
        smax // GS + (heavy - smax + (pdev - 1) * (GS - 1)) // GS,
        (light + pdev * (GS - 1)) // GS,
    )
    rows = GS * atoms
    front = (groups + 1) // 2
    halves = ((0, front), (front, groups - front))
    dims = (nodes, tensors, groups, halves, steps, smax, pdev)
    vmem = pl.BlockSpec(memory_space=pltpu.VMEM)
    smem = pl.BlockSpec(memory_space=pltpu.SMEM)
    return pl.pallas_call(
        functools.partial(kernel, dims),
        out_shape=jax.ShapeDtypeStruct((WORK, flat), F32),
        in_specs=[smem] + [vmem] * 10,
        out_specs=vmem,
        scratch_shapes=[
            pltpu.VMEM((pdev * smax // GS, GS, flat), F32),
            pltpu.VMEM((pdev * pairs, 2 * HEAD, 2 * residues), BF16),
            pltpu.VMEM((pdev * pairs, 2 * residues, 4 * HEAD), BF16),
            pltpu.VMEM((steps, 128, width), BF16),
            pltpu.VMEM((local, 128), BF16),
            pltpu.VMEM((groups * rows, 128), F32),
            pltpu.VMEM((groups * rows, width), BF16),
            pltpu.VMEM((groups * rows, local), BF16),
            pltpu.VMEM((groups * rows, local), BF16),
            pltpu.VMEM((steps, tensors, groups * rows, 128), F32),
            pltpu.VMEM((nodes, 1, flat), F32),
            pltpu.VMEM((nodes, 1, flat), F32),
            pltpu.SemaphoreType.DMA((steps, 2, max(tensors - 1, 1))),
            pltpu.SemaphoreType.DMA((steps, 2, max(tensors - 1, 1))),
            pltpu.SemaphoreType.DMA((nodes - 1,)),
            pltpu.SemaphoreType.DMA((nodes - 1,)),
        ],
        compiler_params=pltpu.CompilerParams(
            collective_id=0, has_side_effects=True, vmem_limit_bytes=60 * 1024 * 1024
        ),
        name="denoise",
    )(
        counts, counts.reshape(1, -1), table, z_home, keys, values, w_embed, step_bias,
        ln_gain.reshape(1, -1), w_query, w_out,
    )


def solution(mesh):
    return jax.shard_map(
        per_device,
        mesh=mesh,
        in_specs=(
            P("pocket", None, None),
            P(),
            P(),
            P("pocket", "tensor", None),
            P("pocket", "tensor", None),
            P(),
            P(),
            P(),
            P("tensor", None),
            P("tensor", None),
        ),
        out_specs=P("pocket", None),
        check_vma=False,
    )
```

profile of v0, /device:TPU:0, one launch (start us, length us, event | category | flops | bytes accessed | tf_op | source)
XLA Modules:
  0.0 60.8 jit_solution(6382158361513828444)
XLA Ops:
  0.0 1.3 %reshape.7.gain_ref = f32[1,1536]{1,0:T(1,128)} reshape(f32[1536]{0:T(1024)} %param.17) | data formatting | bytes 12288 | tf_op jit(solution)/shard_map/reshape | solution.py:326
  1.3 1.4 %copy.11.table_ref = s32[48,32]{1,0:T(8,128)} copy(s32[48,32]{0,1:T(8,128)} %param.12) | data formatting | bytes 12288 | tf_op args[2]
  2.7 1.5 %copy.12.w_out_ref = bf16[768,16]{1,0:T(8,128)(2,1)} copy(bf16[768,16]{0,1:T(8,128)(2,1)} %param.19) | data formatting | bytes 49152 | tf_op args[9]
  4.2 55.2 %denoise.1 = f32[36,256]{1,0:T(8,128)} custom-call(s32[48]{0:T(128)} %counts_s.1, s32[1,48]{1,0:T(1,128)} %bitcast.1, s32[48,32]{1,0:T(8,128)} %copy.11.table_ref, bf16[3,32,256]{2,1,0:T(8,128)(2,1)} %z_home_ref.1, bf16[3,768,128]{2,1,0:T(8,128)(2,1)} %keys_ref.1, bf16[3,768,128]{2,1,0:T(8,128)(2,1)} %values_ref.1, f32[16,1536]{1,0:T(8,128)} %w_embed_ref.1, ...), custom_call_target="tpu_custom_call" | custom-call | tf_op jit(solution)/shard_map/denoise/pallas_call | solution.py:297
  59.4 1.4 %copy.14 = f32[36,256]{1,0:T(8,128)} copy(f32[36,256]{1,0:T(8,128)} %denoise.1) | data formatting | bytes 73728
where the time goes:
time: 61.2 us; the launch traced here: 60.8 us
  Pallas kernels  55.2 us (90%)
  local copies, waits for them, and re-layouts  5.64 us (9%)
    pallas_call x1, Pallas kernels, per_device(): pl.pallas_call(functools.partial(kernel, dims), out_shape=jax.ShapeDtypeS...  55.2 us
    unnamed x3, local copies, waits for them, and re-layouts  4.35 us
    reshape x1, local copies, waits for them, and re-layouts, per_device(): ln_gain.reshape(1, -1)  1.29 us

commit v1 on v0

--- a/solution.py
+++ b/solution.py
@@ -32,9 +32,9 @@
 
 def kernel(
     dims,
-    counts_s, counts_v, table_ref, z_home_ref, keys_ref, values_ref, w_embed_ref, step_bias_ref,
-    gain_ref, w_query_ref, w_out_ref, out_ref,
-    zf, kbd, vbd, wr, wo, z_ref, normed, queries, attended, part, send, recv,
+    counts_s, counts_v, table_ref, z_home_ref, keys_hbm, values_hbm, w_embed_ref, step_bias_ref,
+    gain_ref, w_query_hbm, w_out_ref, out_ref,
+    keys_ref, values_ref, w_query_ref, load, table_s, zf, kbd, vbd, wr, wo, z_ref, normed, queries, attended, part, send, recv,
     psend, precv, fsend, frecv,
 ):
     nodes, tensors, groups, halves, steps, smax, pdev = dims
@@ -54,6 +54,15 @@
         pl.semaphore_signal(barrier, 1, device_id=(lax.rem(me + k, nodes), mt), device_id_type=pl.DeviceIdType.MESH)
     for k in range(1, tensors):
         pl.semaphore_signal(barrier, 1, device_id=(me, lax.rem(mt + k, tensors)), device_id_type=pl.DeviceIdType.MESH)
+
+    loads = [
+        pltpu.make_async_copy(source, target, load.at[k])
+        for k, (source, target) in enumerate(
+            ((keys_hbm, keys_ref), (values_hbm, values_ref), (w_query_hbm, w_query_ref))
+        )
+    ]
+    for copy in loads:
+        copy.start()
 
     tops = []
     total = 0
@@ -86,29 +95,11 @@
         wr[t, 6 * channels:7 * channels, :] = block.astype(BF16)
         wr[t, 7 * channels:, :] = jnp.zeros((128 - 7 * channels, width), BF16)
     spread = (iota((channels, 128), 0) == lax.rem(iota((channels, 128), 1), channels)).astype(BF16)
-    wo[...] = jnp.dot(w_out_ref[...], spread, preferred_element_type=F32).astype(BF16)
+    wo[...] = lax.dot_general(spread, w_out_ref[...], TN, preferred_element_type=F32).astype(BF16)
 
     residues = keys_ref.shape[2]
-    top = iota((2 * HEAD, residues), 0) < HEAD
-    ones = (
-        (iota((2 * residues, 2 * HEAD), 0) < residues) == (iota((2 * residues, 2 * HEAD), 1) < HEAD)
-    ).astype(F32).astype(BF16)
-
-    def prepare(i, carry):
-        p = i // pairs
-        hp = lax.rem(i, pairs)
-        start = pl.multiple_of(hp * 2 * HEAD, 2 * HEAD)
-        k_pair = keys_ref[p, pl.ds(start, 2 * HEAD), :].astype(F32) * 0.125
-        kbd[i, :, :residues] = jnp.where(top, k_pair, 0.0).astype(BF16)
-        kbd[i, :, residues:] = jnp.where(top, 0.0, k_pair).astype(BF16)
-        v_pair = values_ref[p, pl.ds(start, 2 * HEAD), :].astype(F32)
-        vbd[i, :residues, :2 * HEAD] = jnp.where(top, v_pair, 0.0).T.astype(BF16)
-        vbd[i, residues:, :2 * HEAD] = jnp.where(top, 0.0, v_pair).T.astype(BF16)
-        vbd[i, :, 2 * HEAD:] = ones
-        return carry
-
-    lax.fori_loop(0, pdev * pairs, prepare, 0)
-
+    zeros = jnp.zeros((HEAD, residues), BF16)
+    ones = jnp.ones((HEAD, residues), BF16)
     for p in range(pdev):
         block = z_home_ref[p].astype(F32)
         for j in range(per):
@@ -124,88 +115,7 @@
         copies = jnp.where(own_atom, copies, 0.0).astype(BF16)
         z_ref[g * rows:(g + 1) * rows, :] = jnp.dot(copies, fold, preferred_element_type=F32)
 
-    pl.semaphore_wait(barrier, nodes + tensors - 2)
-
-    lane = iota((rows, 128), 1)
-    gain = gain_ref[...]
-
-    def exchange(t, h, k):
-        first, count = halves[h]
-        here = part.at[t, mt, first * rows:(first + count) * rows, :]
-        return pltpu.make_async_remote_copy(
-            src_ref=here, dst_ref=here, send_sem=psend.at[t, h, k - 1], recv_sem=precv.at[t, h, k - 1],
-            device_id=(me, lax.rem(mt + k, tensors)), device_id_type=pl.DeviceIdType.MESH,
-        )
-
-    def pick(t, table):
-        value = jnp.float32(table[-1])
-        for k in range(steps - 1):
-            value = jnp.where(t == k, jnp.float32(table[k]), value)
-        return value
-
-    keeps = [0.95 + 0.01 * k for k in range(steps)]
-    pushes = [-0.8 + 0.1 * k for k in range(steps)]
-
-    def update(t, h):
-        first, count = halves[h]
-        for k in range(1, tensors):
-            exchange(t, h, k).wait()
-        window = slice(first * rows, (first + count) * rows)
-        guess = part[t, 0, window, :]
-        for k in range(1, tensors):
-            guess = guess + part[t, k, window, :]
-        z_ref[window, :] = pick(t, keeps) * z_ref[window, :] + pick(t, pushes) * guess
-
-    def compute(t, h):
-        first, count = halves[h]
-
-        def embed(i, carry):
-            start = pl.multiple_of((first + i) * rows, rows)
-            high, middle, low = split3(z_ref[pl.ds(start, rows), :])
-            left = jnp.where(lane < 3 * channels, high, jnp.where(lane < 5 * channels, middle, jnp.where(lane < 6 * channels, low, 1.0)))
-            centred = jnp.dot(left.astype(BF16), wr[t], preferred_element_type=F32)
-            variance = jnp.sum(centred * centred, axis=1, keepdims=True) * (1.0 / width)
-            normed[pl.ds(start, rows), :] = (centred * lax.rsqrt(variance + EPS) * gain).astype(BF16)
-            return carry
-
-        lax.fori_loop(0, count, embed, 0)
-        window = slice(first * rows, (first + count) * rows)
-        queries[window, :] = lax.dot_general(
-            normed[window, :], w_query_ref[...], NT, preferred_element_type=F32
-        ).astype(BF16)
-
-        def attend(i, carry):
-            g = first + i
-            start = pl.multiple_of(g * rows, rows)
-            pocket, _ = place(g)
-            for hp in range(pairs):
-                cols = slice(hp * 2 * HEAD, (hp + 1) * 2 * HEAD)
-                scores = jnp.dot(queries[pl.ds(start, rows), cols], kbd[pocket * pairs + hp], preferred_element_type=F32)
-                s0 = scores[:, :residues]
-                s1 = scores[:, residues:]
-                e0 = jnp.exp(s0 - jnp.max(s0, axis=1, keepdims=True))
-                e1 = jnp.exp(s1 - jnp.max(s1, axis=1, keepdims=True))
-                e = jnp.concatenate([e0.astype(BF16), e1.astype(BF16)], axis=1)
-                mixed = jnp.dot(e, vbd[pocket * pairs + hp], preferred_element_type=F32)
-                attended[pl.ds(start, rows), cols] = (mixed[:, :2 * HEAD] / mixed[:, 2 * HEAD:]).astype(BF16)
-            return carry
-
-        lax.fori_loop(0, count, attend, 0)
-        part[t, mt, window, :] = jnp.dot(attended[window, :], wo[...], preferred_element_type=F32)
-        for k in range(1, tensors):
-            exchange(t, h, k).start()
-
-    for h in range(len(halves)):
-        compute(0, h)
-
-    def step(t, carry):
-        for h in range(len(halves)):
-            update(t - 1, h)
-            compute(t, h)
-        return carry
-
-    lax.fori_loop(1, steps, step, 0)
-
+    table_s[...] = table_ref[...].astype(F32).T.astype(jnp.int32)
     seats = groups * GS
     slots = -(-WORK // 8) * 8
     lanes = iota((1, seats), 1)
@@ -217,7 +127,7 @@
     keep_rows = jnp.zeros((slots, seats), F32)
     send_rows = jnp.zeros((nodes, seats), F32)
     for p in range(pdev):
-        target = table_ref[pl.ds(me * pdev + p, 1), :]
+        target = table_s[pl.ds(me * pdev + p, 1), :]
         alive = iota((1, smax), 1) < counts_s[me * pdev + p]
         target = jnp.where(alive, target, -1)
         matches = (iota((smax, seats), 0) + p * smax == entry).astype(F32)
@@ -228,7 +138,7 @@
         send_rows = send_rows + jnp.dot(leave.astype(F32), matches, preferred_element_type=F32)
     diagonal = iota((pockets, pockets), 0) == iota((pockets, pockets), 1)
     count_rows = jnp.sum(jnp.where(diagonal, counts_v[...].astype(F32), 0.0), axis=1, keepdims=True)
-    here = table_ref[...] - me * WORK
+    here = table_s[...] - me * WORK
     whose = iota((pockets, smax), 0)
     arrives = (
         (iota((pockets, smax), 1).astype(F32) < count_rows)
@@ -241,6 +151,107 @@
     node_id = iota((pockets, nodes), 1) * pdev
     by_node = ((pocket_id >= node_id) & (pocket_id < node_id + pdev)).astype(F32)
     take_rows = lax.dot_general(by_pocket, by_node, TN, preferred_element_type=F32)
+
+    loads[0].wait()
+    loads[1].wait()
+    for p in range(pdev):
+        for hp in range(pairs):
+            i = p * pairs + hp
+            for side in range(2):
+                inner = slice(side * HEAD, (side + 1) * HEAD)
+                outer = slice(hp * 2 * HEAD + side * HEAD, hp * 2 * HEAD + (side + 1) * HEAD)
+                mine = slice(side * residues, (side + 1) * residues)
+                other = slice((1 - side) * residues, (2 - side) * residues)
+                kbd[i, inner, mine] = keys_ref[p, outer, :] * jnp.asarray(0.125, BF16)
+                kbd[i, inner, other] = zeros
+                vbd[i, inner, mine] = values_ref[p, outer, :]
+                vbd[i, inner, other] = zeros
+                below = slice(2 * HEAD + side * HEAD, 2 * HEAD + (side + 1) * HEAD)
+                vbd[i, below, mine] = ones
+                vbd[i, below, other] = zeros
+
+    loads[2].wait()
+    pl.semaphore_wait(barrier, nodes + tensors - 2)
+
+    lane = iota((rows, 128), 1)
+    gain = gain_ref[...].reshape(1, width)
+
+    def exchange(t, h, k):
+        first, count = halves[h]
+        here = part.at[t, mt, first * rows:(first + count) * rows, :]
+        return pltpu.make_async_remote_copy(
+            src_ref=here, dst_ref=here, send_sem=psend.at[t, h, k - 1], recv_sem=precv.at[t, h, k - 1],
+            device_id=(me, lax.rem(mt + k, tensors)), device_id_type=pl.DeviceIdType.MESH,
+        )
+
+    def pick(t, table):
+        value = jnp.float32(table[-1])
+        for k in range(steps - 1):
+            value = jnp.where(t == k, jnp.float32(table[k]), value)
+        return value
+
+    keeps = [0.95 + 0.01 * k for k in range(steps)]
+    pushes = [-0.8 + 0.1 * k for k in range(steps)]
+
+    def update(t, h):
+        first, count = halves[h]
+        for k in range(1, tensors):
+            exchange(t, h, k).wait()
+        window = slice(first * rows, (first + count) * rows)
+        guess = part[t, 0, window, :]
+        for k in range(1, tensors):
+            guess = guess + part[t, k, window, :]
+        z_ref[window, :] = pick(t, keeps) * z_ref[window, :] + pick(t, pushes) * guess
+
+    def compute(t, h):
+        first, count = halves[h]
+
+        def embed(i):
+            start = (first + i) * rows
+            high, middle, low = split3(z_ref[pl.ds(start, rows), :])
+            left = jnp.where(lane < 3 * channels, high, jnp.where(lane < 5 * channels, middle, jnp.where(lane < 6 * channels, low, 1.0)))
+            centred = jnp.dot(left.astype(BF16), wr[t], preferred_element_type=F32)
+            variance = jnp.sum(centred * centred, axis=1, keepdims=True) * (1.0 / width)
+            normed[pl.ds(start, rows), :] = (centred * lax.rsqrt(variance + EPS) * gain).astype(BF16)
+
+        for i in range(count):
+            embed(i)
+        window = slice(first * rows, (first + count) * rows)
+        queries[window, :] = lax.dot_general(
+            normed[window, :], w_query_ref[...], NT, preferred_element_type=F32
+        ).astype(BF16)
+
+        def attend(i):
+            g = first + i
+            start = g * rows
+            pocket, _ = place(g)
+            for hp in range(pairs):
+                cols = slice(hp * 2 * HEAD, (hp + 1) * 2 * HEAD)
+                scores = jnp.dot(queries[pl.ds(start, rows), cols], kbd[pocket * pairs + hp], preferred_element_type=F32)
+                s0 = scores[:, :residues]
+                s1 = scores[:, residues:]
+                e0 = jnp.exp(s0 - jnp.max(s0, axis=1, keepdims=True))
+                e1 = jnp.exp(s1 - jnp.max(s1, axis=1, keepdims=True))
+                e = jnp.concatenate([e0.astype(BF16), e1.astype(BF16)], axis=1)
+                mixed = lax.dot_general(e, vbd[pocket * pairs + hp], NT, preferred_element_type=F32)
+                attended[pl.ds(start, rows), cols] = (mixed[:, :2 * HEAD] / mixed[:, 2 * HEAD:]).astype(BF16)
+
+        for i in range(count):
+            attend(i)
+        part[t, mt, window, :] = lax.dot_general(attended[window, :], wo[...], NT, preferred_element_type=F32)
+        for k in range(1, tensors):
+            exchange(t, h, k).start()
+
+    for h in range(len(halves)):
+        compute(0, h)
+
+    def step(t, carry):
+        for h in range(len(halves)):
+            update(t - 1, h)
+            compute(t, h)
+        return carry
+
+    lax.fori_loop(1, steps, step, 0)
 
     for h in range(len(halves)):
         update(steps - 1, h)
@@ -294,17 +305,23 @@
     dims = (nodes, tensors, groups, halves, steps, smax, pdev)
     vmem = pl.BlockSpec(memory_space=pltpu.VMEM)
     smem = pl.BlockSpec(memory_space=pltpu.SMEM)
+    hbm = pl.BlockSpec(memory_space=pl.ANY)
     return pl.pallas_call(
         functools.partial(kernel, dims),
         out_shape=jax.ShapeDtypeStruct((WORK, flat), F32),
-        in_specs=[smem] + [vmem] * 10,
+        in_specs=[smem] + [vmem] * 3 + [hbm] * 2 + [vmem] * 3 + [hbm, vmem],
         out_specs=vmem,
         scratch_shapes=[
+            pltpu.VMEM(keys.shape, BF16),
+            pltpu.VMEM(values.shape, BF16),
+            pltpu.VMEM(w_query.shape, BF16),
+            pltpu.SemaphoreType.DMA((3,)),
+            pltpu.VMEM(table.shape, jnp.int32),
             pltpu.VMEM((pdev * smax // GS, GS, flat), F32),
             pltpu.VMEM((pdev * pairs, 2 * HEAD, 2 * residues), BF16),
-            pltpu.VMEM((pdev * pairs, 2 * residues, 4 * HEAD), BF16),
+            pltpu.VMEM((pdev * pairs, 4 * HEAD, 2 * residues), BF16),
             pltpu.VMEM((steps, 128, width), BF16),
-            pltpu.VMEM((local, 128), BF16),
+            pltpu.VMEM((128, local), BF16),
             pltpu.VMEM((groups * rows, 128), F32),
             pltpu.VMEM((groups * rows, width), BF16),
             pltpu.VMEM((groups * rows, local), BF16),
@@ -322,8 +339,8 @@
         ),
         name="denoise",
     )(
-        counts, counts.reshape(1, -1), table, z_home, keys, values, w_embed, step_bias,
-        ln_gain.reshape(1, -1), w_query, w_out,
+        counts, counts.reshape(1, -1), table.T, z_home, keys, values, w_embed, step_bias,
+        ln_gain, w_query, w_out.T,
     )
 
 

time: 61.2 us -> 57.1 us (0.933)
  local copies, waits for them, and re-layouts: 5.64 us -> 1.4 us
    unnamed x3 -> x1, local copies, waits for them, and re-layouts: 4.35 us -> 1.4 us
    reshape x1 -> x0, local copies, waits for them, and re-layouts: 1.29 us -> none  [per_device(): ln_gain.reshape(1, -1)]
where the time goes in v1:
time: 57.1 us; the launch traced here: 56.9 us
  Pallas kernels  55.5 us (97%)
  local copies, waits for them, and re-layouts  1.4 us (2%)
    pallas_call x1, Pallas kernels, per_device(): pl.pallas_call(functools.partial(kernel, dims), out_shape=jax.ShapeDtypeS...  55.5 us
    unnamed x1, local copies, waits for them, and re-layouts  1.4 us

profile of v1, /device:TPU:0, one launch (start us, length us, event | category | flops | bytes accessed | tf_op | source)
XLA Modules:
  0.0 56.9 jit_solution(4147363605622686036)
XLA Ops:
  0.0 55.5 %denoise.1 = f32[36,256]{1,0:T(8,128)} custom-call(s32[48]{0:T(128)} %counts_s.1, s32[1,48]{1,0:T(1,128)} %bitcast.5, s32[32,48]{1,0:T(8,128)} %bitcast.4, bf16[3,32,256]{2,1,0:T(8,128)(2,1)} %z_home_ref.1, bf16[3,768,128]{2,1,0:T(8,128)(2,1)} %keys_hbm.1, bf16[3,768,128]{2,1,0:T(8,128)(2,1)} %values_hbm.1, f32[16,1536]{1,0:T(8,128)} %w_embed_ref.1, ...), custom_call_target="tpu_custom_call" | custom-call | tf_op jit(solution)/shard_map/denoise/pallas_call | solution.py:309
  55.5 1.4 %copy.12 = f32[36,256]{1,0:T(8,128)} copy(f32[36,256]{1,0:T(8,128)} %denoise.1) | data formatting | bytes 73728

commit v2 on v1

--- a/solution.py
+++ b/solution.py
@@ -34,7 +34,7 @@
     dims,
     counts_s, counts_v, table_ref, z_home_ref, keys_hbm, values_hbm, w_embed_ref, step_bias_ref,
     gain_ref, w_query_hbm, w_out_ref, out_ref,
-    keys_ref, values_ref, w_query_ref, load, table_s, zf, kbd, vbd, wr, wo, z_ref, normed, queries, attended, part, send, recv,
+    keys_ref, values_ref, w_query_ref, load, table_s, zf, kbd, vbd, wr, gains, z_ref, normed, queries, attended, part, send, recv,
     psend, precv, fsend, frecv,
 ):
     nodes, tensors, groups, halves, steps, smax, pdev = dims
@@ -83,23 +83,15 @@
     w_full = w_embed_ref[...]
     w_mid = w_full - jnp.mean(w_full, axis=1, keepdims=True)
     a, b, c = split3(w_mid)
-    w_six = [v.astype(BF16) for v in (a, b, c, a, b, a)]
-    bias = step_bias_ref[...]
-    bias = bias - jnp.mean(bias, axis=1, keepdims=True)
-    ba, bb, bc = split3(bias)
-    row_id = iota((channels, width), 0)
-    for t in range(steps):
-        for k in range(6):
-            wr[t, k * channels:(k + 1) * channels, :] = w_six[k]
-        block = jnp.where(row_id == 0, ba[t:t + 1], jnp.where(row_id == 1, bb[t:t + 1], jnp.where(row_id == 2, bc[t:t + 1], 0.0)))
-        wr[t, 6 * channels:7 * channels, :] = block.astype(BF16)
-        wr[t, 7 * channels:, :] = jnp.zeros((128 - 7 * channels, width), BF16)
-    spread = (iota((channels, 128), 0) == lax.rem(iota((channels, 128), 1), channels)).astype(BF16)
-    wo[...] = lax.dot_general(spread, w_out_ref[...], TN, preferred_element_type=F32).astype(BF16)
+    ba, bb, bc = split3(step_bias_ref[...] - jnp.mean(step_bias_ref[...], axis=1, keepdims=True))
+    padding = jnp.zeros((128 - 6 * channels - 3 * steps, width), F32)
+    stacked = jnp.concatenate([a, b, c, a, b, a, ba, bb, bc, padding], axis=0)
+    wr[...] = stacked.T.astype(BF16)
+    gains[...] = jnp.broadcast_to(gain_ref[...].reshape(1, width), (128, width)).T
 
     residues = keys_ref.shape[2]
     zeros = jnp.zeros((HEAD, residues), BF16)
-    ones = jnp.ones((HEAD, residues), BF16)
+    left_head = iota((residues, 2 * HEAD), 1) < HEAD
     for p in range(pdev):
         block = z_home_ref[p].astype(F32)
         for j in range(per):
@@ -107,13 +99,13 @@
 
     flat = atoms * channels
     own_atom = iota((rows, flat), 1) // channels == lax.rem(iota((rows, flat), 0), atoms)
-    fold = (lax.rem(iota((flat, 128), 0), channels) == lax.rem(iota((flat, 128), 1), channels)).astype(BF16)
+    fold = (lax.rem(iota((channels, flat), 1), channels) == iota((channels, flat), 0)).astype(F32)
     for g in range(groups):
         pocket, block = place(jnp.int32(g))
         flat_z = zf[block]
         copies = jnp.broadcast_to(flat_z[:, None, :], (GS, atoms, flat)).reshape(rows, flat)
         copies = jnp.where(own_atom, copies, 0.0).astype(BF16)
-        z_ref[g * rows:(g + 1) * rows, :] = jnp.dot(copies, fold, preferred_element_type=F32)
+        z_ref[:, g * rows:(g + 1) * rows] = lax.dot_general(fold.astype(BF16), copies, NT, preferred_element_type=F32)
 
     table_s[...] = table_ref[...].astype(F32).T.astype(jnp.int32)
     seats = groups * GS
@@ -157,28 +149,22 @@
     for p in range(pdev):
         for hp in range(pairs):
             i = p * pairs + hp
+            turned = (keys_ref[p, hp * 2 * HEAD:(hp + 1) * 2 * HEAD, :].astype(F32) * 0.125).T
+            kbd[i, :residues, :] = jnp.where(left_head, turned, 0.0).astype(BF16)
+            kbd[i, residues:, :] = jnp.where(left_head, 0.0, turned).astype(BF16)
             for side in range(2):
                 inner = slice(side * HEAD, (side + 1) * HEAD)
                 outer = slice(hp * 2 * HEAD + side * HEAD, hp * 2 * HEAD + (side + 1) * HEAD)
-                mine = slice(side * residues, (side + 1) * residues)
-                other = slice((1 - side) * residues, (2 - side) * residues)
-                kbd[i, inner, mine] = keys_ref[p, outer, :] * jnp.asarray(0.125, BF16)
-                kbd[i, inner, other] = zeros
-                vbd[i, inner, mine] = values_ref[p, outer, :]
-                vbd[i, inner, other] = zeros
-                below = slice(2 * HEAD + side * HEAD, 2 * HEAD + (side + 1) * HEAD)
-                vbd[i, below, mine] = ones
-                vbd[i, below, other] = zeros
+                vbd[i, inner, side * residues:(side + 1) * residues] = values_ref[p, outer, :]
+                vbd[i, inner, (1 - side) * residues:(2 - side) * residues] = zeros
 
     loads[2].wait()
     pl.semaphore_wait(barrier, nodes + tensors - 2)
 
-    lane = iota((rows, 128), 1)
-    gain = gain_ref[...].reshape(1, width)
 
     def exchange(t, h, k):
         first, count = halves[h]
-        here = part.at[t, mt, first * rows:(first + count) * rows, :]
+        here = part.at[t, mt, :, first * rows:(first + count) * rows]
         return pltpu.make_async_remote_copy(
             src_ref=here, dst_ref=here, send_sem=psend.at[t, h, k - 1], recv_sem=precv.at[t, h, k - 1],
             device_id=(me, lax.rem(mt + k, tensors)), device_id_type=pl.DeviceIdType.MESH,
@@ -198,47 +184,49 @@
         for k in range(1, tensors):
             exchange(t, h, k).wait()
         window = slice(first * rows, (first + count) * rows)
-        guess = part[t, 0, window, :]
+        guess = part[t, 0, :, window]
         for k in range(1, tensors):
-            guess = guess + part[t, k, window, :]
-        z_ref[window, :] = pick(t, keeps) * z_ref[window, :] + pick(t, pushes) * guess
+            guess = guess + part[t, k, :, window]
+        z_ref[:, window] = pick(t, keeps) * z_ref[:, window] + pick(t, pushes) * guess
 
     def compute(t, h):
         first, count = halves[h]
 
-        def embed(i):
-            start = (first + i) * rows
-            high, middle, low = split3(z_ref[pl.ds(start, rows), :])
-            left = jnp.where(lane < 3 * channels, high, jnp.where(lane < 5 * channels, middle, jnp.where(lane < 6 * channels, low, 1.0)))
-            centred = jnp.dot(left.astype(BF16), wr[t], preferred_element_type=F32)
-            variance = jnp.sum(centred * centred, axis=1, keepdims=True) * (1.0 / width)
-            normed[pl.ds(start, rows), :] = (centred * lax.rsqrt(variance + EPS) * gain).astype(BF16)
-
-        for i in range(count):
-            embed(i)
         window = slice(first * rows, (first + count) * rows)
-        queries[window, :] = lax.dot_general(
-            normed[window, :], w_query_ref[...], NT, preferred_element_type=F32
-        ).astype(BF16)
-
-        def attend(i):
-            g = first + i
-            start = g * rows
-            pocket, _ = place(g)
+        for start in range(first, first + count, 2):
+            span = min(2, first + count - start)
+            some = slice(start * rows, (start + span) * rows)
+            high, middle, low = split3(z_ref[:, some])
+            rest_id = iota((128 - 6 * channels, span * rows), 0)
+            flags = ((lax.rem(rest_id, steps) == t) & (rest_id < 3 * steps)).astype(F32)
+            right = jnp.concatenate([high, high, high, middle, middle, low, flags], axis=0).astype(BF16)
+            centred = jnp.dot(wr[...], right, preferred_element_type=F32)
+            variance = jnp.sum(centred * centred, axis=0, keepdims=True) * (1.0 / width)
+            scale = lax.rsqrt(variance + EPS)
+            for k in range(span):
+                part_k = slice(k * rows, (k + 1) * rows)
+                normed[:, (start + k) * rows:(start + k + 1) * rows] = (
+                    centred[:, part_k] * scale[:, part_k] * gains[...]
+                ).astype(BF16)
+        queries[:, window] = jnp.dot(w_query_ref[...], normed[:, window], preferred_element_type=F32).astype(BF16)
+
+        for g in range(first, first + count):
+            lanes_g = slice(g * rows, (g + 1) * rows)
+            pocket, _ = place(jnp.int32(g))
             for hp in range(pairs):
                 cols = slice(hp * 2 * HEAD, (hp + 1) * 2 * HEAD)
-                scores = jnp.dot(queries[pl.ds(start, rows), cols], kbd[pocket * pairs + hp], preferred_element_type=F32)
-                s0 = scores[:, :residues]
-                s1 = scores[:, residues:]
-                e0 = jnp.exp(s0 - jnp.max(s0, axis=1, keepdims=True))
-                e1 = jnp.exp(s1 - jnp.max(s1, axis=1, keepdims=True))
-                e = jnp.concatenate([e0.astype(BF16), e1.astype(BF16)], axis=1)
-                mixed = lax.dot_general(e, vbd[pocket * pairs + hp], NT, preferred_element_type=F32)
-                attended[pl.ds(start, rows), cols] = (mixed[:, :2 * HEAD] / mixed[:, 2 * HEAD:]).astype(BF16)
-
-        for i in range(count):
-            attend(i)
-        part[t, mt, window, :] = lax.dot_general(attended[window, :], wo[...], NT, preferred_element_type=F32)
+                scores = jnp.dot(kbd[pocket * pairs + hp], queries[cols, lanes_g], preferred_element_type=F32)
+                s0 = scores[:residues]
+                s1 = scores[residues:]
+                e0 = jnp.exp(s0 - jnp.max(s0, axis=0, keepdims=True))
+                e1 = jnp.exp(s1 - jnp.max(s1, axis=0, keepdims=True))
+                r0 = 1.0 / jnp.sum(e0, axis=0, keepdims=True)
+                r1 = 1.0 / jnp.sum(e1, axis=0, keepdims=True)
+                e = jnp.concatenate([e0.astype(BF16), e1.astype(BF16)], axis=0)
+                mixed = jnp.dot(vbd[pocket * pairs + hp], e, preferred_element_type=F32)
+                attended[hp * 2 * HEAD:hp * 2 * HEAD + HEAD, lanes_g] = (mixed[:HEAD] * r0).astype(BF16)
+                attended[hp * 2 * HEAD + HEAD:(hp + 1) * 2 * HEAD, lanes_g] = (mixed[HEAD:] * r1).astype(BF16)
+        part[t, mt, :, window] = jnp.dot(w_out_ref[...], attended[:, window], preferred_element_type=F32)
         for k in range(1, tensors):
             exchange(t, h, k).start()
 
@@ -257,8 +245,9 @@
         update(steps - 1, h)
     done = []
     for g in range(groups):
-        z = z_ref[g * rows:(g + 1) * rows, :]
-        wide = jnp.concatenate([z] * (flat // 128), axis=1)
+        wide = lax.dot_general(
+            z_ref[:, g * rows:(g + 1) * rows], fold, TN, precision=HIGHEST, preferred_element_type=F32
+        )
         done.append(jnp.sum(jnp.where(own_atom, wide, 0.0).reshape(GS, atoms, flat), axis=1))
     done = jnp.concatenate(done, axis=0)
     leaving = jnp.dot(send_rows, done, precision=HIGHEST, preferred_element_type=F32)
@@ -318,15 +307,15 @@
             pltpu.SemaphoreType.DMA((3,)),
             pltpu.VMEM(table.shape, jnp.int32),
             pltpu.VMEM((pdev * smax // GS, GS, flat), F32),
+            pltpu.VMEM((pdev * pairs, 2 * residues, 2 * HEAD), BF16),
             pltpu.VMEM((pdev * pairs, 2 * HEAD, 2 * residues), BF16),
-            pltpu.VMEM((pdev * pairs, 4 * HEAD, 2 * residues), BF16),
-            pltpu.VMEM((steps, 128, width), BF16),
-            pltpu.VMEM((128, local), BF16),
-            pltpu.VMEM((groups * rows, 128), F32),
-            pltpu.VMEM((groups * rows, width), BF16),
-            pltpu.VMEM((groups * rows, local), BF16),
-            pltpu.VMEM((groups * rows, local), BF16),
-            pltpu.VMEM((steps, tensors, groups * rows, 128), F32),
+            pltpu.VMEM((width, 128), BF16),
+            pltpu.VMEM((width, 128), F32),
+            pltpu.VMEM((channels, groups * rows), F32),
+            pltpu.VMEM((width, groups * rows), BF16),
+            pltpu.VMEM((local, groups * rows), BF16),
+            pltpu.VMEM((local, groups * rows), BF16),
+            pltpu.VMEM((steps, tensors, channels, groups * rows), F32),
             pltpu.VMEM((nodes, 1, flat), F32),
             pltpu.VMEM((nodes, 1, flat), F32),
             pltpu.SemaphoreType.DMA((steps, 2, max(tensors - 1, 1))),

time: 57.1 us -> 49.9 us (0.87)
  Pallas kernels: 55.5 us -> 48.3 us
    pallas_call x1, Pallas kernels: 55.5 us -> 48.3 us  [per_device(): pl.pallas_call(functools.partial(kernel, dims), out_shape=jax.ShapeDtypeS...]
where the time goes in v2:
time: 49.9 us; the launch traced here: 49.7 us
  Pallas kernels  48.3 us (97%)
  local copies, waits for them, and re-layouts  1.4 us (3%)
    pallas_call x1, Pallas kernels, per_device(): pl.pallas_call(functools.partial(kernel, dims), out_shape=jax.ShapeDtypeS...  48.3 us
    unnamed x1, local copies, waits for them, and re-layouts  1.4 us

profile of v2, /device:TPU:0, one launch (start us, length us, event | category | flops | bytes accessed | tf_op | source)
XLA Modules:
  0.0 49.7 jit_solution(15640525074845530631)
XLA Ops:
  0.0 48.3 %denoise.1 = f32[36,256]{1,0:T(8,128)} custom-call(s32[48]{0:T(128)} %counts_s.1, s32[1,48]{1,0:T(1,128)} %bitcast.5, s32[32,48]{1,0:T(8,128)} %bitcast.4, bf16[3,32,256]{2,1,0:T(8,128)(2,1)} %z_home_ref.1, bf16[3,768,128]{2,1,0:T(8,128)(2,1)} %keys_hbm.1, bf16[3,768,128]{2,1,0:T(8,128)(2,1)} %values_hbm.1, f32[16,1536]{1,0:T(8,128)} %w_embed_ref.1, ...), custom_call_target="tpu_custom_call" | custom-call | tf_op jit(solution)/shard_map/denoise/pallas_call | solution.py:298
  48.3 1.4 %copy.12 = f32[36,256]{1,0:T(8,128)} copy(f32[36,256]{1,0:T(8,128)} %denoise.1) | data formatting | bytes 73728

commit v3 on v2

--- a/solution.py
+++ b/solution.py
@@ -80,14 +80,18 @@
         block = jnp.clip(g - first, 0, per - 1)
         return pocket, pocket * per + block
 
-    w_full = w_embed_ref[...]
-    w_mid = w_full - jnp.mean(w_full, axis=1, keepdims=True)
-    a, b, c = split3(w_mid)
-    ba, bb, bc = split3(step_bias_ref[...] - jnp.mean(step_bias_ref[...], axis=1, keepdims=True))
-    padding = jnp.zeros((128 - 6 * channels - 3 * steps, width), F32)
-    stacked = jnp.concatenate([a, b, c, a, b, a, ba, bb, bc, padding], axis=0)
-    wr[...] = stacked.T.astype(BF16)
-    gains[...] = jnp.broadcast_to(gain_ref[...].reshape(1, width), (128, width)).T
+    w_mid = w_embed_ref[...] - jnp.mean(w_embed_ref[...], axis=1, keepdims=True)
+    bias = step_bias_ref[...] - jnp.mean(step_bias_ref[...], axis=1, keepdims=True)
+    gain = gain_ref[...].reshape(1, width)
+    padding = jnp.zeros((128 - 6 * (channels + steps), width), F32)
+
+    def stack(weights, biases):
+        a, b, c = split3(weights)
+        ba, bb, bc = split3(biases)
+        return jnp.concatenate([a, b, c, a, b, a, ba, bb, bc, ba, bb, ba, padding], axis=0).T.astype(BF16)
+
+    wr[...] = stack(w_mid, bias)
+    gains[...] = stack(w_mid * gain, bias * gain)
 
     residues = keys_ref.shape[2]
     zeros = jnp.zeros((HEAD, residues), BF16)
@@ -200,13 +204,22 @@
             rest_id = iota((128 - 6 * channels, span * rows), 0)
             flags = ((lax.rem(rest_id, steps) == t) & (rest_id < 3 * steps)).astype(F32)
             right = jnp.concatenate([high, high, high, middle, middle, low, flags], axis=0).astype(BF16)
-            centred = jnp.dot(wr[...], right, preferred_element_type=F32)
-            variance = jnp.sum(centred * centred, axis=0, keepdims=True) * (1.0 / width)
-            scale = lax.rsqrt(variance + EPS)
-            for k in range(span):
-                part_k = slice(k * rows, (k + 1) * rows)
-                normed[:, (start + k) * rows:(start + k + 1) * rows] = (
-                    centred[:, part_k] * scale[:, part_k] * gains[...]
+            total_sq = jnp.zeros((1, span * rows), F32)
+            chunk = width // 4
+            for f in range(0, width, chunk):
+                centred = jnp.dot(wr[f:f + chunk, :], right, preferred_element_type=F32)
+                total_sq = total_sq + jnp.sum(centred * centred, axis=0, keepdims=True)
+            scale = lax.rsqrt(total_sq * (1.0 / width) + EPS)
+            high, middle, low = split3(z_ref[:, some] * scale)
+            s_high, s_middle, s_low = split3(scale)
+            scales = jnp.where(rest_id < 3 * steps, s_high, jnp.where(rest_id < 5 * steps, s_middle, s_low))
+            mine = (lax.rem(rest_id, steps) == t) & (rest_id < 6 * steps)
+            right = jnp.concatenate(
+                [high, high, high, middle, middle, low, jnp.where(mine, scales, 0.0)], axis=0
+            ).astype(BF16)
+            for f in range(0, width, chunk):
+                normed[f:f + chunk, some] = jnp.dot(
+                    gains[f:f + chunk, :], right, preferred_element_type=F32
                 ).astype(BF16)
         queries[:, window] = jnp.dot(w_query_ref[...], normed[:, window], preferred_element_type=F32).astype(BF16)
 
@@ -310,7 +323,7 @@
             pltpu.VMEM((pdev * pairs, 2 * residues, 2 * HEAD), BF16),
             pltpu.VMEM((pdev * pairs, 2 * HEAD, 2 * residues), BF16),
             pltpu.VMEM((width, 128), BF16),
-            pltpu.VMEM((width, 128), F32),
+            pltpu.VMEM((width, 128), BF16),
             pltpu.VMEM((channels, groups * rows), F32),
             pltpu.VMEM((width, groups * rows), BF16),
             pltpu.VMEM((local, groups * rows), BF16),

time: 49.9 us -> 45.6 us (0.914)
  Pallas kernels: 48.3 us -> 43.9 us
    pallas_call x1, Pallas kernels: 48.3 us -> 43.9 us  [per_device(): pl.pallas_call(functools.partial(kernel, dims), out_shape=jax.ShapeDtypeS...]
where the time goes in v3:
time: 45.6 us; the launch traced here: 45.4 us
  Pallas kernels  43.9 us (96%)
  local copies, waits for them, and re-layouts  1.4 us (3%)
    pallas_call x1, Pallas kernels, per_device(): pl.pallas_call(functools.partial(kernel, dims), out_shape=jax.ShapeDtypeS...  43.9 us
    unnamed x1, local copies, waits for them, and re-layouts  1.4 us

profile of v3, /device:TPU:0, one launch (start us, length us, event | category | flops | bytes accessed | tf_op | source)
XLA Modules:
  0.0 45.4 jit_solution(8420241990365332799)
XLA Ops:
  0.0 43.9 %denoise.1 = f32[36,256]{1,0:T(8,128)} custom-call(s32[48]{0:T(128)} %counts_s.1, s32[1,48]{1,0:T(1,128)} %bitcast.5, s32[32,48]{1,0:T(8,128)} %bitcast.4, bf16[3,32,256]{2,1,0:T(8,128)(2,1)} %z_home_ref.1, bf16[3,768,128]{2,1,0:T(8,128)(2,1)} %keys_hbm.1, bf16[3,768,128]{2,1,0:T(8,128)(2,1)} %values_hbm.1, f32[16,1536]{1,0:T(8,128)} %w_embed_ref.1, ...), custom_call_target="tpu_custom_call" | custom-call | tf_op jit(solution)/shard_map/denoise/pallas_call | solution.py:311
  44.0 1.4 %copy.12 = f32[36,256]{1,0:T(8,128)} copy(f32[36,256]{1,0:T(8,128)} %denoise.1) | data formatting | bytes 73728
